TPU v7x, 256 devices: a whole 4x4x8 slice. The times are simulated.
256 devices in a mesh: rep: 4 (over z_hi), dom: 64 (over y, x, z_lo, core).
Axes of the slice: x: 4, y: 4, z: 8 (z_hi: 4, z_lo: 2; z = z_hi * 2 + z_lo), core: 2. Of those that a mesh axis runs over, the one named last changes fastest.
Arguments:
- cols: int32 [512, 8], P('dom', 'rep'), may hold values from 0 to 511, as said below
- vals: bfloat16 [512, 8, 128, 128], P('dom', 'rep')
- features: bfloat16 [65536, 128], P(('rep', 'dom')), may hold values from -6 to 6
- weight: bfloat16 [128, 128], replicated, may hold values from -0.5 to 0.5
- bias: float32 [128], replicated, may hold values from -3 to 3
- cotangent: bfloat16 [65536, 128], P('dom'), may hold values from -6 to 6
Outputs:
- output: bfloat16 [65536, 128], P('dom')
- feature_grad: float32 [65536, 128], P(('rep', 'dom'))
- weight_grad: float32 [128, 128], replicated
Inputs may be any that keep to these rules, and one draw needn't show every extreme that they name: For every block row and every quarter q of the block columns, entries q * 2 to (q + 1) * 2 - 1 of its row of cols are 2 distinct block columns in the range q * 128 to (q + 1) * 128 - 1 (quarters as many as the size of rep); every block row names its own diagonal block.
All inputs are finite; a program needn't handle non-finite values.
Results may differ from a plain program's by a relative error of at most 0.0055.
Values may be sent and summed in bfloat16 or wider, within the bound.
A program may use at most 64 MiB of HBM per device.

v0:
```python
import jax
import jax.numpy as jnp
from jax import lax
from jax.sharding import PartitionSpec as P


def body(cols, vals, features, weight, bias, cotangent):
    row_blocks, block_count, block_size, _ = vals.shape
    width = features.shape[1]
    quarter_blocks = features.shape[0] * lax.axis_size("dom") // block_size
    local_cols = cols - lax.axis_index("rep") * quarter_blocks
    quarter = lax.all_gather(features, "dom", axis=0, tiled=True).reshape(
        quarter_blocks, block_size, width
    )
    picked = quarter[local_cols]
    partial_sum = jnp.einsum("rkij,rkjf->rif", vals, picked, preferred_element_type=jnp.float32)
    partial_sum = partial_sum.reshape(row_blocks * block_size, width)
    summed = lax.psum(partial_sum, "rep")
    aggregated = summed.astype(jnp.bfloat16)
    hidden = jnp.dot(aggregated, weight, preferred_element_type=jnp.float32) + bias
    gate_prob = jax.nn.sigmoid(hidden)
    output = (hidden * gate_prob).astype(jnp.bfloat16)
    grad_hidden = (
        cotangent.astype(jnp.float32) * gate_prob * (1.0 + hidden * (1.0 - gate_prob))
    ).astype(jnp.bfloat16)
    weight_part = lax.dot_general(
        aggregated, grad_hidden, (((0,), (0,)), ((), ())), preferred_element_type=jnp.float32
    )
    grad_agg = lax.dot_general(
        grad_hidden, weight, (((1,), (1,)), ((), ())), preferred_element_type=jnp.float32
    ).astype(jnp.bfloat16)
    weight_grad = lax.psum(weight_part, "dom")
    full_output, full_grad = (output, grad_agg)
    grad_blocks = full_grad.reshape(row_blocks, block_size, width)
    terms = jnp.einsum("rkij,rif->rkjf", vals, grad_blocks, preferred_element_type=jnp.float32)
    flat_terms = terms.reshape(row_blocks * block_count, block_size, width)
    flat_cols = local_cols.reshape(-1)
    contrib = jax.ops.segment_sum(flat_terms, flat_cols, num_segments=quarter_blocks)
    contrib = contrib.reshape(quarter_blocks * block_size, width)
    feature_grad = lax.psum_scatter(contrib, "dom", scatter_dimension=0, tiled=True)
    return (full_output, feature_grad, weight_grad)


def solution(mesh):
    placed = (
        P("dom", "rep"),
        P("dom", "rep", None, None),
        P(("rep", "dom"), None),
        P(),
        P(),
        P("dom", None),
    )
    return jax.shard_map(
        body,
        mesh=mesh,
        in_specs=placed,
        out_specs=(P("dom", None), P(("rep", "dom"), None), P()),
        check_vma=False,
    )
```

profile of v0, /device:TPU:1, one launch (start us, length us, event | category | flops | bytes accessed | tf_op | source)
XLA Modules:
  0.0 940.9 jit_solution(18369843405789627181)
XLA Ops:
  7.2 0.0 copy-start
  7.2 0.0 all-gather.2.cloned.1.call-start
  7.2 0.7 all-gather.2.cloned.1.call-update
  7.9 0.0 all-reduce.3.cloned.1.call-start
  8.0 0.7 compare_select_fusion
  8.6 0.1 copy.12
  8.7 0.1 reshape.29
  8.8 0.1 copy.13
  8.9 0.1 reshape.37
  9.0 113.6 %all-gather.2.cloned.1.call-done = bf16[16384,128]{1,0:T(8,128)(2,1)} async-done(((bf16[256,128]{1,0:T(8,128)(2,1)}), bf16[16384,128]{1,0:T(8,128)(2,1)}) %all-gather.2.cloned.1.call-update) | async-done | bytes 4194320 | tf_op jit(solution)/shard_map/all_gather | solution.py:12
  122.6 2.8 gather_fusion
  125.4 0.0 copy-done
  125.4 0.3 fusion.4
  125.7 28.0 %all-reduce.4 = bf16[1024,128]{1,0:T(8,128)(2,1)S(1)} all-reduce(f32[1024,128]{1,0:T(8,128)S(1)} %bitcast.30), channel_id=1, replica_groups=mesh['rep'=4,'dom'=64] {'rep'}, use_global_device_ids=true, to_apply=%region_0.0 | all-reduce | flops 131072 | bytes 786432 | tf_op jit(solution)/shard_map/psum | solution.py:18
  153.7 2.1 multiply_convert_fusion
  155.8 0.9 fusion.5
  156.7 1.0 convolution_convert_fusion
  157.7 0.0 all-reduce.3.cloned.1.call-update
  157.7 0.0 reduce-scatter.2.cloned.1.call-start
  157.8 0.3 fusion.3
  158.1 0.3 copy.15
  158.5 4.3 broadcast_in_dim.8
  162.7 3.3 scatter_fusion
  166.1 0.0 reduce-scatter.2.cloned.1.call-update
  166.1 466.9 %all-reduce.3.cloned.1.call-done = f32[128,128]{1,0:T(8,128)} async-done(((f32[128,128]{1,0:T(8,128)}), f32[128,128]{1,0:T(8,128)}) %all-reduce.3.cloned.1.call-update) | async-done | bytes 65552 | tf_op jit(solution)/shard_map/psum | solution.py:32
  633.0 299.9 %reduce-scatter.2.cloned.1.call-done = f32[256,128]{1,0:T(8,128)} async-done(((f32[16384,128]{1,0:T(8,128)}), f32[256,128]{1,0:T(8,128)}) %reduce-scatter.2.cloned.1.call-update) | async-done | bytes 131088 | tf_op jit(solution)/shard_map/reduce_scatter | solution.py:40
  932.9 1.5 copy.24
  (1 shorter events, 0.0 us)
Async XLA Ops:
  7.2 118.2 %copy-start = (bf16[8,2,128,128]{3,2,1,0:T(8,128)(2,1)S(1)}, bf16[8,2,128,128]{3,2,1,0:T(8,128)(2,1)}, u32[]{:S(2)}) copy-start(bf16[8,2,128,128]{3,2,1,0:T(8,128)(2,1)} %param.7) | copy-start | bytes 1572868
  7.2 115.4 %all-gather.2.cloned.1.call-start = ((), (), s32[]{:S(2)}) async-start(), calls=%async_computation.1 | async-start | bytes 4259840 | tf_op jit(solution)/shard_map/all_gather | solution.py:12
  7.9 625.1 %all-reduce.3.cloned.1.call-start = ((), (), s32[]{:S(2)}) async-start(), calls=%async_computation.3 | async-start | bytes 131072 | tf_op jit(solution)/shard_map/psum | solution.py:32
  157.7 775.2 %reduce-scatter.2.cloned.1.call-start = ((), (), s32[]{:S(2)}) async-start(), calls=%async_computation.2 | async-start | bytes 8519680 | tf_op jit(solution)/shard_map/reduce_scatter | solution.py:40
Sparse Core Ops, SparseCore 0:
  9.9 112.6 all-gather.1
  157.8 475.0 all-reduce.2
  636.2 296.6 reduce-scatter.1
where the time goes:
time: 944 us; the launch traced here: 941 us
  waiting for transfers between devices  881 us (93%)
  blocking collectives  28 us (3%)
  between operations  13.8 us (1%)
    psum x1, waiting for transfers between devices, body(): weight_grad = lax.psum(weight_part, 'dom')  467 us
    reduce_scatter x1, waiting for transfers between devices, body(): lax.psum_scatter(contrib, 'dom', scatter_dimension=0, tiled=True)  300 us
    all_gather x1, waiting for transfers between devices, body(): lax.all_gather(features, 'dom', axis=0, tiled=True)  114 us
    psum x1, blocking collectives, body(): summed = lax.psum(partial_sum, 'rep')  28 us
  transfers between devices with their start and end apart: 3, of which 3 were waited for; matrix products, arithmetic and copies ran while one was open for 1% of the time, Pallas kernels for 0%

commit v1 on v0

v1 whole, which is shorter than its diff:
```python
import jax
import jax.numpy as jnp
from jax import lax
from jax.experimental import pallas as pl
from jax.experimental.pallas import tpu as pltpu
from jax.sharding import PartitionSpec as P

MESH = pl.DeviceIdType.MESH
F32 = jnp.float32
BF16 = jnp.bfloat16
BS = 128
ORDER = (2, 1, 3, 0)
SENDS = 200


def kernel(
    cols_ref, vals_ref, feat_ref, weight_ref, bias_ref, cot_ref,
    out_ref, fgrad_ref, wgrad_ref,
    cols_s, first_s, next_s,
    vals_v, vals_t, weight_v, bias_v, cot_v, first_v,
    quart, part, part_in, agg, grad, out_v,
    wpart, wsib, wa, wb, wz, wr, wfull,
    acc, acc_b, acc_sib,
    dense, relay_in, final_in, summed, relay2_in, final2_in, tail, tail_b, tail_in, fg_v,
    load_sem, send_sem, ag_sem, agsib_sem, tab_sem, rep_sem, repag_sem, w_sem, accsib_sem,
    relay_sem, final_sem, relay2_sem, final2_sem, tail_sem,
):
    rep = lax.axis_index("rep")
    dom = lax.axis_index("dom")
    y, x, z, c = dom // 16, (dom // 4) % 4, (dom // 2) % 2, dom % 2
    pa = x + c * (y - x)
    pb = y + c * (x - y)

    def flat(qa, qb, qz):
        qx = qa + c * (qb - qa)
        qy = qb + c * (qa - qb)
        return (qy * 4 + qx) * 2 + qz

    def off(da, db):
        return (pa + da) % 4, (pb + db) % 4

    def device(da=0, db=0, qz=None, core=None, drep=0):
        qa, qb = off(da, db)
        i = flat(qa, qb, z if qz is None else qz)
        return ((rep + drep) % 4, i * 2 + (c if core is None else core))

    sib = device(core=1 - c)
    zpeer = device(qz=1 - z)
    started = []

    def send(src, dst, sem, target):
        n = len(started)
        copy = pltpu.make_async_remote_copy(
            src_ref=src, dst_ref=dst, send_sem=send_sem.at[n], recv_sem=sem, device_id=target, device_id_type=MESH
        )
        copy.start()
        started.append(copy)

    def arrive(dst, sem):
        pltpu.make_async_remote_copy(
            src_ref=dst, dst_ref=dst, send_sem=send_sem.at[0], recv_sem=sem, device_id=sib, device_id_type=MESH
        ).wait_recv()

    loads = []

    def load(src, dst):
        copy = pltpu.make_async_copy(src, dst, load_sem.at[len(loads)])
        copy.start()
        loads.append(copy)
        return copy

    own = flat(pa, pb, z)
    own_slot = quart.at[pl.ds((own * 2 + c) * 2, 2)]
    load_cols = load(cols_ref, cols_s)
    load_feat = load(feat_ref, own_slot)
    load_vals = load(vals_ref, vals_v)
    load_weight = load(weight_ref, weight_v)
    load_bias = load(bias_ref, bias_v)
    load_cot = load(cot_ref, cot_v)

    barrier = pltpu.get_barrier_semaphore()
    partners = [sib, zpeer]
    partners += [device(da=k) for k in (1, 2, 3)]
    partners += [device(db=k) for k in (1, 2, 3)]
    partners += [device(drep=k) for k in (1, 2, 3)]
    for partner in partners:
        pl.semaphore_signal(barrier, inc=1, device_id=partner, device_id_type=MESH)
    pl.semaphore_wait(barrier, len(partners))

    def shard(i):
        return quart.at[pl.ds((i * 2 + c) * 2, 2)]

    def half(i, h):
        return quart.at[pl.ds((i * 2 + c) * 2 + h, 1)]

    def to_axis(i, da, db, src=None):
        send(shard(i) if src is None else src, shard(i), ag_sem.at[i, 0], device(da=da, db=db))

    def to_sib(i, src=None):
        send(shard(i) if src is None else src, shard(i), agsib_sem.at[i], sib)

    def got(i):
        arrive(shard(i), ag_sem.at[i, 0])

    def got_half(i, h):
        arrive(half(i, h), ag_sem.at[i, h])

    for da, db in ((0, 1), (0, 3), (1, 0), (3, 0)):
        to_axis(own, da, db, feat_ref)
    send(feat_ref, shard(own), ag_sem.at[own, 0], zpeer)
    to_sib(own, feat_ref)

    load_cols.wait()
    column = [lax.rem(cols_s[t % 2, t // 2], 128) for t in range(16)]
    lane = lax.broadcasted_iota(jnp.int32, (1, 128), 1)
    first = jnp.full((1, 128), 16, jnp.int32)
    for t in reversed(range(16)):
        first = jnp.where(lane == column[t], t, first)
    first_v[0] = first
    send(first_v.at[0], first_v.at[1], tab_sem, sib)

    def a_shard(da, qz):
        i = flat((pa + da) % 4, pb, qz)
        if da == 2:
            got_half(i, 0)
            got_half(i, 1)
        else:
            got(i)
            h, onward = (0, 1) if da == 3 else (1, 3)
            send(half(i, h), half(i, h), ag_sem.at[i, h], device(da=onward))
        to_axis(i, 0, 1)
        to_axis(i, 0, 3)
        to_sib(i)

    def b_shard(da, db, qz):
        qa, qb = off(da, db)
        i = flat(qa, qb, qz)
        if db == 2:
            got_half(i, 0)
            got_half(i, 1)
        else:
            got(i)
            h, onward = (0, 1) if db == 3 else (1, 3)
            send(half(i, h), half(i, h), ag_sem.at[i, h], device(db=onward))
        to_sib(i)

    across = flat(pa, pb, 1 - z)
    got(across)
    for da, db in ((0, 1), (0, 3), (1, 0), (3, 0)):
        to_axis(across, da, db)
    to_sib(across)
    a_shard(3, z)
    a_shard(1, z)
    b_shard(0, 3, z)
    b_shard(0, 1, z)
    a_shard(3, 1 - z)
    a_shard(1, 1 - z)
    b_shard(0, 3, 1 - z)
    b_shard(0, 1, 1 - z)
    a_shard(2, z)
    a_shard(2, 1 - z)

    load_vals.wait()

    def transpose(t):
        vals_t[t] = vals_v[t].T

    todo = list(range(16))
    for da, qz in ((3, z), (1, z), (3, 1 - z), (1, 1 - z), (2, z), (2, 1 - z)):
        for db in (3, 1):
            b_shard(da, db, qz)
            if todo:
                transpose(todo.pop(0))
    for t in range(16):
        following = jnp.int32(16)
        for u in reversed(range(t + 1, 16)):
            if u // 2 != t // 2:
                following = jnp.where(column[u] == column[t], u, following)
        next_s[t] = following
    for da in (0, 3, 1, 2):
        for qz in (z, 1 - z):
            b_shard(da, 2, qz)
            if todo:
                transpose(todo.pop(0))
    acc[16] = jnp.zeros((BS, BS), F32)
    acc_b[16] = jnp.zeros((BS, BS), BF16)
    acc_sib[16] = jnp.zeros((BS, BS), BF16)
    arrive(first_v.at[1], tab_sem)
    table_copy = pltpu.make_async_copy(first_v, first_s, load_sem.at[6])
    table_copy.start()
    load_feat.wait()
    for i in range(32):
        arrive(quart.at[pl.ds((i * 2 + 1 - c) * 2, 2)], agsib_sem.at[i])

    def row_sum(row):
        left = jnp.dot(vals_v[row * 2], quart[lax.rem(cols_s[0, row], 128)], preferred_element_type=F32)
        right = jnp.dot(vals_v[row * 2 + 1], quart[lax.rem(cols_s[1, row], 128)], preferred_element_type=F32)
        return left + right

    own_sum = []
    for k in ORDER:
        s = (rep + k) % 4
        for j in range(2):
            total = row_sum(s * 2 + j)
            if k == 0:
                own_sum.append(total)
            else:
                part[k, j] = total.astype(BF16)
        if k:
            send(part.at[k], part_in.at[k], rep_sem.at[k], device(drep=k))
    for k in (1, 3, 2):
        arrive(part_in.at[k], rep_sem.at[k])
    for j in range(2):
        total = own_sum[j] + (
            part_in[1, j].astype(F32) + part_in[3, j].astype(F32) + part_in[2, j].astype(F32)
        )
        agg[rep, pl.ds(j * BS, BS)] = total.astype(BF16)
    for k in (2, 1, 3):
        send(agg.at[rep], agg.at[rep], repag_sem.at[k], device(drep=k))

    load_weight.wait()
    load_bias.wait()
    load_cot.wait()
    stores = []

    def store(src, dst):
        copy = pltpu.make_async_copy(src, dst, load_sem.at[7 + len(stores)])
        copy.start()
        stores.append(copy)

    def layer(s):
        rows = agg[s]
        hidden = jnp.dot(rows, weight_v[...], preferred_element_type=F32) + bias_v[...]
        gate = jax.nn.sigmoid(hidden)
        out_v[s] = (hidden * gate).astype(BF16)
        grad_hidden = (cot_v[s].astype(F32) * gate * (1.0 + hidden * (1.0 - gate))).astype(BF16)
        grad_rows = lax.dot_general(
            grad_hidden, weight_v[...], (((1,), (1,)), ((), ())), preferred_element_type=F32
        )
        grad[s] = grad_rows.astype(BF16)
        store(out_v.at[s], out_ref.at[s])
        return rows, grad_hidden

    rows, grad_hidden = layer(rep)
    product = lax.dot_general(rows, grad_hidden, (((0,), (0,)), ((), ())), preferred_element_type=F32)
    wpart[0] = product[:64]
    wpart[1] = product[64:]
    send(wpart.at[1 - c], wsib, w_sem.at[0], sib)
    for k in (3, 1, 2):
        arrive(agg.at[(rep + 4 - k) % 4], repag_sem.at[k])
        layer((rep + 4 - k) % 4)

    def w_stage_a():
        arrive(wsib, w_sem.at[0])
        wa[pa] = wpart[c] + wsib[...]
        for k in (1, 2, 3):
            send(wa.at[pa], wa.at[pa], w_sem.at[k], device(da=k))

    def w_stage_b():
        for k in (1, 2, 3):
            arrive(wa.at[(pa + 4 - k) % 4], w_sem.at[k])
        wb[pb] = (wa[0] + wa[1]) + (wa[2] + wa[3])
        for k in (1, 2, 3):
            send(wb.at[pb], wb.at[pb], w_sem.at[3 + k], device(db=k))

    def w_stage_z():
        for k in (1, 2, 3):
            arrive(wb.at[(pb + 4 - k) % 4], w_sem.at[3 + k])
        wz[z] = (wb[0] + wb[1]) + (wb[2] + wb[3])
        send(wz.at[z], wz.at[z], w_sem.at[7], zpeer)

    def w_stage_rep():
        arrive(wz.at[1 - z], w_sem.at[7])
        wr[rep] = wz[0] + wz[1]
        for k in (1, 2, 3):
            send(wr.at[rep], wr.at[rep], w_sem.at[7 + k], device(drep=k))

    def w_stage_sib():
        for k in (1, 2, 3):
            arrive(wr.at[(rep + 4 - k) % 4], w_sem.at[7 + k])
        wfull[c] = (wr[0] + wr[1]) + (wr[2] + wr[3])
        send(wfull.at[c], wfull.at[c], w_sem.at[11], sib)

    def w_done():
        arrive(wfull.at[1 - c], w_sem.at[11])
        store(wfull, wgrad_ref)

    w_stage_a()

    for t in reversed(range(16)):
        row = t // 2
        term = jnp.dot(vals_t[t], grad[row // 2, pl.ds((row % 2) * BS, BS)], preferred_element_type=F32)
        term = term + acc[next_s[t]]
        acc[t] = term
        acc_b[t] = term.astype(BF16)
        if t % 4 == 0:
            send(acc_b.at[pl.ds(t, 4)], acc_sib.at[pl.ds(t, 4)], accsib_sem.at[t // 4], sib)
    table_copy.wait()
    w_stage_b()
    for q in range(4):
        arrive(acc_sib.at[pl.ds(q * 4, 4)], accsib_sem.at[q])

    def place(ob, oa, blk=0, zz=0):
        return ((ob * 4 + oa) * 2 + blk) * 2 + zz

    def build(ob, oa):
        qa, qb = off(oa, ob)
        for blk in range(2):
            for zz in range(2):
                j = (flat(qa, qb, zz) * 2 + c) * 2 + blk
                dense[place(ob, oa, blk, zz)] = acc_b[first_s[0, 0, j]] + acc_sib[first_s[1, 0, j]]

    def pair(ob, oa, blk):
        return dense.at[pl.ds(place(ob, oa, blk), 2)]

    for oa in ORDER:
        build(2, oa)
        send(pair(2, oa, 0), relay_in.at[0, oa], relay_sem.at[0, oa], device(db=1))
        send(pair(2, oa, 1), relay_in.at[1, oa], relay_sem.at[1, oa], device(db=3))
    for oa in ORDER:
        build(1, oa)
        send(pair(1, oa, 1), final_in.at[0, oa, 1], final_sem.at[0, oa, 1], device(db=1))
        build(3, oa)
        send(pair(3, oa, 0), final_in.at[1, oa, 0], final_sem.at[1, oa, 0], device(db=3))
    for oa in ORDER:
        for side, ob, blk in ((0, 1, 0), (1, 3, 1)):
            arrive(relay_in.at[side, oa], relay_sem.at[side, oa])
            at = pl.ds(place(ob, oa, blk), 2)
            dense[at] = (dense[at].astype(F32) + relay_in[side, oa].astype(F32)).astype(BF16)
            send(pair(ob, oa, blk), final_in.at[side, oa, blk], final_sem.at[side, oa, blk], device(db=ob))
    w_stage_z()
    for oa in ORDER:
        build(0, oa)

    def sum_b(oa):
        for side in range(2):
            for blk in range(2):
                arrive(final_in.at[side, oa, blk], final_sem.at[side, oa, blk])
        for blk in range(2):
            total = dense[pl.ds(place(0, oa, blk), 2)].astype(F32) + (
                final_in[0, oa, blk].astype(F32) + final_in[1, oa, blk].astype(F32)
            )
            summed[oa, blk] = total.astype(BF16)

    sum_b(2)
    send(summed.at[2, 0], relay2_in.at[0], relay2_sem.at[0], device(da=1))
    send(summed.at[2, 1], relay2_in.at[1], relay2_sem.at[1], device(da=3))
    w_stage_rep()
    sum_b(1)
    send(summed.at[1, 1], final2_in.at[0, 1], final2_sem.at[0, 1], device(da=1))
    sum_b(3)
    send(summed.at[3, 0], final2_in.at[1, 0], final2_sem.at[1, 0], device(da=3))
    for side, oa, blk in ((0, 1, 0), (1, 3, 1)):
        arrive(relay2_in.at[side], relay2_sem.at[side])
        summed[oa, blk] = (summed[oa, blk].astype(F32) + relay2_in[side].astype(F32)).astype(BF16)
        send(summed.at[oa, blk], final2_in.at[side, blk], final2_sem.at[side, blk], device(da=oa))
    sum_b(0)
    w_stage_sib()
    for side in range(2):
        for blk in range(2):
            arrive(final2_in.at[side, blk], final2_sem.at[side, blk])
    for blk in range(2):
        for zz in range(2):
            total = summed[0, blk, zz].astype(F32) + (
                final2_in[0, blk, zz].astype(F32) + final2_in[1, blk, zz].astype(F32)
            )
            tail[zz, blk] = total
            tail_b[zz, blk] = total.astype(BF16)
    send(tail_b.at[1 - z], tail_in, tail_sem, zpeer)
    w_done()
    arrive(tail_in, tail_sem)
    fg_v[...] = tail[z] + tail_in[...].astype(F32)
    store(fg_v, fgrad_ref)
    for copy in started:
        copy.wait_send()
    for copy in stores:
        copy.wait()


def body(cols, vals, features, weight, bias, cotangent):
    anywhere = pl.BlockSpec(memory_space=pl.ANY)
    vmem = pltpu.VMEM
    dma = pltpu.SemaphoreType.DMA
    block = (BS, BS)
    scratch = [
        pltpu.SMEM((2, 8), jnp.int32),
        pltpu.SMEM((2, 1, 128), jnp.int32),
        pltpu.SMEM((16,), jnp.int32),
        vmem((16, *block), BF16),
        vmem((16, *block), BF16),
        vmem(block, BF16),
        vmem((1, BS), F32),
        vmem((4, 256, BS), BF16),
        vmem((2, 1, 128), jnp.int32),
        vmem((128, *block), BF16),
        vmem((4, 2, *block), BF16),
        vmem((4, 2, *block), BF16),
        vmem((4, 256, BS), BF16),
        vmem((4, 256, BS), BF16),
        vmem((4, 256, BS), BF16),
        vmem((2, 64, BS), F32),
        vmem((64, BS), F32),
        vmem((4, 64, BS), F32),
        vmem((4, 64, BS), F32),
        vmem((2, 64, BS), F32),
        vmem((4, 64, BS), F32),
        vmem((2, 64, BS), F32),
        vmem((17, *block), F32),
        vmem((17, *block), BF16),
        vmem((17, *block), BF16),
        vmem((64, *block), BF16),
        vmem((2, 4, 2, *block), BF16),
        vmem((2, 4, 2, 2, *block), BF16),
        vmem((4, 2, 2, *block), BF16),
        vmem((2, 2, *block), BF16),
        vmem((2, 2, 2, *block), BF16),
        vmem((2, 2, *block), F32),
        vmem((2, 2, *block), BF16),
        vmem((2, *block), BF16),
        vmem((2, *block), F32),
        dma((16,)),
        dma((SENDS,)),
        dma((32, 2)),
        dma((32,)),
        dma,
        dma((4,)),
        dma((4,)),
        dma((12,)),
        dma((4,)),
        dma((2, 4)),
        dma((2, 4, 2)),
        dma((2,)),
        dma((2, 2)),
        dma,
    ]
    output, feature_grad, weight_grad = pl.pallas_call(
        kernel,
        out_shape=(
            jax.ShapeDtypeStruct((4, 256, BS), BF16),
            jax.ShapeDtypeStruct((2, *block), F32),
            jax.ShapeDtypeStruct((2, 64, BS), F32),
        ),
        in_specs=[anywhere] * 6,
        out_specs=(anywhere,) * 3,
        scratch_shapes=scratch,
        compiler_params=pltpu.CompilerParams(
            collective_id=0, has_side_effects=True, vmem_limit_bytes=32 << 20
        ),
    )(
        cols.T,
        vals.reshape(16, *block),
        features.reshape(2, *block),
        weight,
        bias.reshape(1, BS),
        cotangent.reshape(4, 256, BS),
    )
    return output.reshape(1024, BS), feature_grad.reshape(256, BS), weight_grad.reshape(BS, BS)


def solution(mesh):
    placed = (
        P("dom", "rep"),
        P("dom", "rep", None, None),
        P(("rep", "dom"), None),
        P(),
        P(),
        P("dom", None),
    )
    return jax.shard_map(
        body,
        mesh=mesh,
        in_specs=placed,
        out_specs=(P("dom", None), P(("rep", "dom"), None), P()),
        check_vma=False,
    )
```

time: 944 us -> 81.8 us (0.09)
  the two profiles are of different devices: /device:TPU:1 before, /device:TPU:2 now
where the time goes in v1:
time: 81.8 us; the launch traced here: 81.5 us
  Pallas kernels  74.6 us (91%)
  local copies, waits for them, and re-layouts  6.24 us (8%)
    pallas_call x1, Pallas kernels, body(): pl.pallas_call(kernel, out_shape=(jax.ShapeDtypeStruct((4, 256, BS), BF16...  74.6 us
    unnamed x15, local copies, waits for them, and re-layouts  6.24 us

profile of v1, /device:TPU:2, one launch (start us, length us, event | category | flops | bytes accessed | tf_op | source)
XLA Modules:
  0.0 81.5 jit_solution(7703157973933018580)
XLA Ops:
  0.6 0.0 copy-start.4
  0.6 0.0 copy-start.5
  0.7 0.7 copy-done.4
  1.3 0.0 copy-done.5
  1.3 0.0 copy-start
  1.3 1.0 %copy-done = bf16[8,2,128,128]{3,2,1,0:T(8,128)(2,1)S(1)} copy-done((bf16[8,2,128,128]{3,2,1,0:T(8,128)(2,1)S(1)}, bf16[8,2,128,128]{3,2,1,0:T(8,128)(2,1)}, u32[]{:S(2)}) %copy-start) | copy-done | bytes 524312
  2.4 0.0 copy-start.1
  2.4 0.9 %copy-done.1 = bf16[1024,128]{1,0:T(8,128)(2,1)S(1)} copy-done((bf16[1024,128]{1,0:T(8,128)(2,1)S(1)}, bf16[1024,128]{1,0:T(8,128)(2,1)}, u32[]{:S(2)}) %copy-start.1) | copy-done | bytes 262168
  3.3 0.0 copy-start.2
  3.3 0.8 %copy-done.2 = bf16[256,128]{1,0:T(8,128)(2,1)S(1)} copy-done((bf16[256,128]{1,0:T(8,128)(2,1)S(1)}, bf16[256,128]{1,0:T(8,128)(2,1)}, u32[]{:S(2)}) %copy-start.2) | copy-done | bytes 65560
  4.1 0.0 copy-start.3
  4.2 0.8 copy-done.3
  4.9 74.6 %shard_map.85 = (bf16[4,256,128]{2,1,0:T(8,128)(2,1)S(1)}, f32[2,128,128]{2,1,0:T(8,128)S(1)}, f32[2,64,128]{2,1,0:T(8,128)S(1)}) custom-call(s32[2,8]{1,0:T(2,128)S(1)} %bitcast.14, bf16[16,128,128]{2,1,0:T(8,128)(2,1)S(1)} %bitcast.8, bf16[2,128,128]{2,1,0:T(8,128)(2,1)S(1)} %bitcast.13, bf16[128,128]{1,0:T(8,128)(2,1)S(1)} %copy-done.3, ...), custom_call_target="tpu_custom_call" | custom-call | tf_op jit(solution)/shard_map/pallas_call | solution.py:436
  79.5 0.7 copy.12
  80.2 0.7 copy.13
  80.9 0.6 copy.14
Async XLA Ops:
  0.6 0.7 copy-start.4
  0.6 0.7 copy-start.5
  1.3 1.0 %copy-start = (bf16[8,2,128,128]{3,2,1,0:T(8,128)(2,1)S(1)}, bf16[8,2,128,128]{3,2,1,0:T(8,128)(2,1)}, u32[]{:S(2)}) copy-start(bf16[8,2,128,128]{3,2,1,0:T(8,128)(2,1)} %param.7) | copy-start | bytes 1572868
  2.4 0.9 %copy-start.1 = (bf16[1024,128]{1,0:T(8,128)(2,1)S(1)}, bf16[1024,128]{1,0:T(8,128)(2,1)}, u32[]{:S(2)}) copy-start(bf16[1024,128]{1,0:T(8,128)(2,1)} %param.11) | copy-start | bytes 786436
  3.3 0.8 %copy-start.2 = (bf16[256,128]{1,0:T(8,128)(2,1)S(1)}, bf16[256,128]{1,0:T(8,128)(2,1)}, u32[]{:S(2)}) copy-start(bf16[256,128]{1,0:T(8,128)(2,1)} %param.8) | copy-start | bytes 196612
  4.1 0.8 copy-start.3

commit v2 on v0

v2 whole, which is shorter than its diff:
```python
import jax
import jax.numpy as jnp
from jax import lax
from jax.experimental import pallas as pl
from jax.experimental.pallas import tpu as pltpu
from jax.sharding import PartitionSpec as P

MESH = pl.DeviceIdType.MESH
F32 = jnp.float32
BF16 = jnp.bfloat16
BS = 128
ORDER = (2, 1, 3, 0)
DIRECT = ((2, 1),)


def kernel(
    cols_ref, vals_ref, feat_ref, weight_ref, bias_ref, cot_ref,
    out_ref, fgrad_ref, wgrad_ref,
    cols_s, first_s, next_s,
    vals_v, vals_t, weight_v, bias_v, cot_v, first_v,
    quart, part, part_in, agg, out_v,
    wpart, wsib, wa, wb, wr, wfull,
    acc, acc_b, acc_sib,
    dense, relay_in, final_in, summed, near_in, fg_v,
    load_sem, send_sem, ag_sem, agsib_sem, tab_sem, rep_sem, repag_sem, w_sem, accsib_sem,
    relay_sem, final_sem, near_sem,
):
    rep = lax.axis_index("rep")
    dom = lax.axis_index("dom")
    y, x, z, c = dom // 16, (dom // 4) % 4, (dom // 2) % 2, dom % 2
    pa = x + c * (y - x)
    pb = y + c * (x - y)

    def flat(qa, qb, qz):
        qx = qa + c * (qb - qa)
        qy = qb + c * (qa - qb)
        return (qy * 4 + qx) * 2 + qz

    def spot(da, db, dz):
        return flat((pa + da) % 4, (pb + db) % 4, (z + dz) % 2)

    def device(da=0, db=0, dz=0, core=None, drep=0):
        return ((rep + drep) % 4, spot(da, db, dz) * 2 + (c if core is None else core))

    sib = device(core=1 - c)
    sent = [0, 0, 0]

    def send(src, dst, sem, target, group=2, blocks=1):
        pltpu.make_async_remote_copy(
            src_ref=src, dst_ref=dst, send_sem=send_sem.at[group], recv_sem=sem, device_id=target, device_id_type=MESH
        ).start()
        sent[group] += blocks

    def arrive(dst, sem):
        pltpu.make_async_remote_copy(
            src_ref=dst, dst_ref=dst, send_sem=send_sem.at[0], recv_sem=sem, device_id=sib, device_id_type=MESH
        ).wait_recv()

    loads = []

    def load(src, dst):
        copy = pltpu.make_async_copy(src, dst, load_sem.at[len(loads)])
        copy.start()
        loads.append(copy)
        return copy

    own = spot(0, 0, 0)
    load_feat = load(feat_ref, quart.at[pl.ds((own * 2 + c) * 2, 2)])
    load_cols = load(cols_ref, cols_s)
    load_vals = load(vals_ref, vals_v)
    load_weight = load(weight_ref, weight_v)
    load_bias = load(bias_ref, bias_v)
    load_cot = load(cot_ref, cot_v)

    near = [(1, 0), (3, 0), (0, 1), (2, 0), (1, 1), (3, 1), (2, 1)]
    barrier = pltpu.get_barrier_semaphore()
    partners = [sib]
    partners += [device(da=da, dz=dz) for da, dz in near]
    partners += [device(db=k) for k in (1, 2, 3)]
    partners += [device(drep=k) for k in (1, 2, 3)]
    for partner in partners:
        pl.semaphore_signal(barrier, inc=1, device_id=partner, device_id_type=MESH)
    load_feat.wait()
    pl.semaphore_wait(barrier, len(partners))

    def shard(i):
        return quart.at[pl.ds((i * 2 + c) * 2, 2)]

    def half(i, h):
        return quart.at[pl.ds((i * 2 + c) * 2 + h, 1)]

    def half_sem(i, h):
        return ag_sem.at[h * 32 + i]

    def to_axis(i, **where):
        send(shard(i), shard(i), ag_sem.at[i], device(**where), 1, 2)

    def to_sib(i):
        send(shard(i), shard(i), agsib_sem, sib, 0, 2)

    def along_b(da, dz):
        i = spot(da, 0, dz)
        to_axis(i, db=1)
        to_axis(i, db=3)
        if (da, dz) in DIRECT:
            to_axis(i, db=2)
        to_sib(i)

    along_b(0, 0)
    for da, dz in near:
        to_axis(own, da=da, dz=dz)

    arrivals = [(k, j) for j in range(2) for k in (1, 3, 2)]
    order = ([(0, 0), (0, 1)] + arrivals)[::-1]
    rows = [((rep + 4 - k) % 4) * 2 + j for k, j in order]
    load_cols.wait()
    column = [lax.rem(cols_s[t % 2, rows[t // 2]], 128) for t in range(16)]
    lane = lax.broadcasted_iota(jnp.int32, (1, 128), 1)
    first = jnp.full((1, 128), 16, jnp.int32)
    for t in reversed(range(16)):
        first = jnp.where(lane == column[t], t, first)
    first_v[0] = first
    first_copy = pltpu.make_async_remote_copy(
        src_ref=first_v.at[0], dst_ref=first_v.at[1], send_sem=send_sem.at[3], recv_sem=tab_sem,
        device_id=sib, device_id_type=MESH,
    )
    first_copy.start()

    def near_shard(da, dz):
        i = spot(da, 0, dz)
        arrive(shard(i), ag_sem.at[i])
        along_b(da, dz)

    def beside(da, dz):
        for db, h, onward in ((3, 0, 1), (1, 1, 3)):
            i = spot(da, db, dz)
            arrive(shard(i), ag_sem.at[i])
            if (da, dz) not in DIRECT:
                send(half(i, h), half(i, h), half_sem(i, h), device(db=onward), 1, 1)
            to_sib(i)

    def opposite(da, dz):
        i = spot(da, 2, dz)
        if (da, dz) in DIRECT:
            arrive(shard(i), ag_sem.at[i])
        else:
            arrive(half(i, 0), half_sem(i, 0))
            arrive(half(i, 1), half_sem(i, 1))
        to_sib(i)

    load_vals.wait()
    todo = list(range(16))

    def transpose(n):
        for _ in range(n):
            t = todo.pop(0)
            vals_t[t] = vals_v[rows[t // 2] * 2 + t % 2].T

    transpose(4)
    near_shard(1, 0)
    near_shard(3, 0)
    near_shard(0, 1)
    beside(0, 0)
    near_shard(2, 0)
    near_shard(1, 1)
    near_shard(3, 1)
    beside(1, 0)
    beside(3, 0)
    beside(0, 1)
    near_shard(2, 1)
    transpose(2)
    beside(2, 0)
    transpose(2)
    beside(1, 1)
    transpose(2)
    beside(3, 1)
    transpose(2)
    opposite(0, 0)
    transpose(2)
    opposite(1, 0)
    transpose(2)
    opposite(3, 0)
    for t in range(16):
        following = jnp.int32(16)
        for u in reversed(range(t + 1, 16)):
            if u // 2 != t // 2:
                following = jnp.where(column[u] == column[t], u, following)
        next_s[t] = following
    acc[16] = jnp.zeros((BS, BS), F32)
    acc_b[16] = jnp.zeros((BS, BS), BF16)
    acc_sib[16] = jnp.zeros((BS, BS), BF16)
    arrive(first_v.at[1], tab_sem)
    table_copy = pltpu.make_async_copy(first_v, first_s, load_sem.at[6])
    table_copy.start()
    opposite(0, 1)
    opposite(2, 0)
    beside(2, 1)
    opposite(1, 1)
    opposite(3, 1)
    opposite(2, 1)
    arrive(quart.at[pl.ds(0, 64)], agsib_sem)

    def row_sum(row):
        left = jnp.dot(vals_v[row * 2], quart[lax.rem(cols_s[0, row], 128)], preferred_element_type=F32)
        right = jnp.dot(vals_v[row * 2 + 1], quart[lax.rem(cols_s[1, row], 128)], preferred_element_type=F32)
        return left + right

    own_sum = []
    for j in range(2):
        for k in ORDER:
            total = row_sum(((rep + k) % 4) * 2 + j)
            if k == 0:
                own_sum.append(total)
            else:
                part[k, j] = total.astype(BF16)
                send(part.at[k, j], part_in.at[k, j], rep_sem.at[k, j], device(drep=k))

    def reduce_rep(j):
        for k in (1, 3, 2):
            arrive(part_in.at[k, j], rep_sem.at[k, j])
        total = own_sum[j] + (
            part_in[1, j].astype(F32) + part_in[3, j].astype(F32) + part_in[2, j].astype(F32)
        )
        agg[rep * 2 + j] = total.astype(BF16)
        for k in (2, 1, 3):
            send(agg.at[rep * 2 + j], agg.at[rep * 2 + j], repag_sem.at[k, j], device(drep=k))

    def layer(pos):
        row = rows[pos]
        mine = agg[row]
        hidden = jnp.dot(mine, weight_v[...], preferred_element_type=F32) + bias_v[...]
        gate = jax.nn.sigmoid(hidden)
        out_v[row] = (hidden * gate).astype(BF16)
        pltpu.make_async_copy(out_v.at[row], out_ref.at[row], load_sem.at[7]).start()
        grad_hidden = (cot_v[row].astype(F32) * gate * (1.0 + hidden * (1.0 - gate))).astype(BF16)
        grad_rows = lax.dot_general(
            grad_hidden, weight_v[...], (((1,), (1,)), ((), ())), preferred_element_type=F32
        ).astype(BF16)
        for t in (pos * 2 + 1, pos * 2):
            term = jnp.dot(vals_t[t], grad_rows, preferred_element_type=F32) + acc[next_s[t]]
            acc[t] = term
            acc_b[t] = term.astype(BF16)
        send(acc_b.at[pl.ds(pos * 2, 2)], acc_sib.at[pl.ds(pos * 2, 2)], accsib_sem, sib, 2, 2)
        return lax.dot_general(mine, grad_hidden, (((0,), (0,)), ((), ())), preferred_element_type=F32) if pos > 5 else None

    def w_stage_near():
        arrive(wsib, w_sem.at[0])
        wa[pa * 2 + z] = wpart[c] + wsib[...]
        for n, (da, dz) in enumerate(near):
            send(wa.at[pa * 2 + z], wa.at[pa * 2 + z], w_sem.at[1 + n], device(da=da, dz=dz))

    def w_stage_b():
        for n, (da, dz) in enumerate(near):
            arrive(wa.at[((pa + 4 - da) % 4) * 2 + (z + dz) % 2], w_sem.at[1 + n])
        wb[pb] = ((wa[0] + wa[1]) + (wa[2] + wa[3])) + ((wa[4] + wa[5]) + (wa[6] + wa[7]))
        for k in (1, 2, 3):
            send(wb.at[pb], wb.at[pb], w_sem.at[7 + k], device(db=k))

    def w_stage_rep():
        for k in (1, 2, 3):
            arrive(wb.at[(pb + 4 - k) % 4], w_sem.at[7 + k])
        wr[rep] = (wb[0] + wb[1]) + (wb[2] + wb[3])
        for k in (1, 2, 3):
            send(wr.at[rep], wr.at[rep], w_sem.at[10 + k], device(drep=k))

    def w_stage_sib():
        for k in (1, 2, 3):
            arrive(wr.at[(rep + 4 - k) % 4], w_sem.at[10 + k])
        wfull[c] = (wr[0] + wr[1]) + (wr[2] + wr[3])
        send(wfull.at[c], wfull.at[c], w_sem.at[14], sib)

    load_weight.wait()
    load_bias.wait()
    load_cot.wait()
    reduce_rep(0)
    product = layer(7)
    reduce_rep(1)
    product = product + layer(6)
    wpart[0] = product[:64]
    wpart[1] = product[64:]
    send(wpart.at[1 - c], wsib, w_sem.at[0], sib)
    for n, (k, j) in enumerate(arrivals):
        arrive(agg.at[rows[5 - n]], repag_sem.at[k, j])
        layer(5 - n)
        if n == 1:
            w_stage_near()
    table_copy.wait()
    arrive(acc_sib.at[pl.ds(0, 16)], accsib_sem)

    def place(ob, oa, zz):
        return ((ob * 4 + oa) * 2 + zz) * 2

    def build(ob, oa):
        for zz in range(2):
            i = flat((pa + oa) % 4, (pb + ob) % 4, zz)
            for blk in range(2):
                j = (i * 2 + c) * 2 + blk
                dense[place(ob, oa, zz) + blk] = acc_b[first_s[0, 0, j]] + acc_sib[first_s[1, 0, j]]

    def to_b(oa, ob, zz):
        side = 0 if ob == 1 else 1
        send(
            dense.at[pl.ds(place(ob, oa, zz), 2)], final_in.at[side, oa, zz], final_sem.at[side, oa], device(db=ob), 2, 2
        )

    for oa in ORDER:
        build(2, oa)
        send(dense.at[pl.ds(place(2, oa, 0), 2)], relay_in.at[0, oa], relay_sem.at[0, oa], device(db=1), 2, 2)
        send(dense.at[pl.ds(place(2, oa, 1), 2)], relay_in.at[1, oa], relay_sem.at[1, oa], device(db=3), 2, 2)
    for n, oa in enumerate(ORDER):
        build(1, oa)
        build(3, oa)
        if n == 0:
            to_b(oa, 1, 1)
            to_b(oa, 3, 0)
    w_stage_b()
    for n, oa in enumerate(ORDER):
        for side, ob, zz in ((0, 1, 0), (1, 3, 1)):
            arrive(relay_in.at[side, oa], relay_sem.at[side, oa])
            at = pl.ds(place(ob, oa, zz), 2)
            dense[at] = (dense[at].astype(F32) + relay_in[side, oa].astype(F32)).astype(BF16)
            to_b(oa, ob, zz)
        if n < 3:
            to_b(ORDER[n + 1], 1, 1)
            to_b(ORDER[n + 1], 3, 0)
    for oa in ORDER:
        build(0, oa)

    for oa in ORDER:
        for side in range(2):
            arrive(final_in.at[side, oa], final_sem.at[side, oa])
        for zz in range(2):
            total = dense[pl.ds(place(0, oa, zz), 2)].astype(F32) + (
                final_in[0, oa, zz].astype(F32) + final_in[1, oa, zz].astype(F32)
            )
            summed[oa, zz] = total.astype(BF16)
            if oa == 0:
                fg_v[zz] = total
        for dz in (1, 0):
            if oa or dz:
                slot = oa * 2 + dz
                send(summed.at[oa, (z + dz) % 2], near_in.at[slot], near_sem.at[slot], device(da=oa, dz=dz), 2, 2)
        if oa == 2:
            w_stage_rep()
    w_stage_sib()
    total = fg_v[z]
    for oa in ORDER:
        for dz in (0, 1):
            if oa or dz:
                slot = oa * 2 + dz
                arrive(near_in.at[slot], near_sem.at[slot])
                total = total + near_in[slot].astype(F32)
    fg_v[2] = total
    fgrad_copy = pltpu.make_async_copy(fg_v.at[2], fgrad_ref, load_sem.at[8])
    fgrad_copy.start()
    arrive(wfull.at[1 - c], w_sem.at[14])
    wgrad_copy = pltpu.make_async_copy(wfull, wgrad_ref, load_sem.at[9])
    wgrad_copy.start()
    for group, blocks in enumerate(sent):
        assert blocks <= 128
        ref = quart.at[pl.ds(0, blocks)]
        pltpu.make_async_remote_copy(
            src_ref=ref, dst_ref=ref, send_sem=send_sem.at[group], recv_sem=tab_sem, device_id=sib, device_id_type=MESH
        ).wait_send()
    first_copy.wait_send()
    pltpu.make_async_copy(out_v, out_ref, load_sem.at[7]).wait()
    fgrad_copy.wait()
    wgrad_copy.wait()


def emit(out_in, fgrad_in, wgrad_in, out_ref, fgrad_ref, wgrad_ref, sem):
    copies = [
        pltpu.make_async_copy(src, dst, sem.at[n])
        for n, (src, dst) in enumerate(((out_in, out_ref), (fgrad_in, fgrad_ref), (wgrad_in, wgrad_ref)))
    ]
    for copy in copies:
        copy.start()
    for copy in copies:
        copy.wait()


def body(cols, vals, features, weight, bias, cotangent):
    anywhere = pl.BlockSpec(memory_space=pl.ANY)
    vmem = pltpu.VMEM
    dma = pltpu.SemaphoreType.DMA
    block = (BS, BS)
    scratch = [
        pltpu.SMEM((2, 8), jnp.int32),
        pltpu.SMEM((2, 1, 128), jnp.int32),
        pltpu.SMEM((16,), jnp.int32),
        vmem((16, *block), BF16),
        vmem((16, *block), BF16),
        vmem(block, BF16),
        vmem((1, BS), F32),
        vmem((8, *block), BF16),
        vmem((2, 1, 128), jnp.int32),
        vmem((128, *block), BF16),
        vmem((4, 2, *block), BF16),
        vmem((4, 2, *block), BF16),
        vmem((8, *block), BF16),
        vmem((8, *block), BF16),
        vmem((2, 64, BS), F32),
        vmem((64, BS), F32),
        vmem((8, 64, BS), F32),
        vmem((4, 64, BS), F32),
        vmem((4, 64, BS), F32),
        vmem((2, 64, BS), F32),
        vmem((17, *block), F32),
        vmem((17, *block), BF16),
        vmem((17, *block), BF16),
        vmem((64, *block), BF16),
        vmem((2, 4, 2, *block), BF16),
        vmem((2, 4, 2, 2, *block), BF16),
        vmem((4, 2, 2, *block), BF16),
        vmem((8, 2, *block), BF16),
        vmem((3, 2, *block), F32),
        dma((10,)),
        dma((4,)),
        dma((64,)),
        dma,
        dma,
        dma((4, 2)),
        dma((4, 2)),
        dma((15,)),
        dma,
        dma((2, 4)),
        dma((2, 4)),
        dma((8,)),
    ]
    results = (
        jax.ShapeDtypeStruct((8, *block), BF16),
        jax.ShapeDtypeStruct((2, *block), F32),
        jax.ShapeDtypeStruct((2, 64, BS), F32),
    )
    operands = (
        cols.T,
        vals.reshape(16, *block),
        features.reshape(2, *block),
        weight,
        bias.reshape(1, BS),
        cotangent.reshape(8, *block),
    )
    outs = pl.pallas_call(
        kernel,
        out_shape=results,
        in_specs=[anywhere] * 6,
        out_specs=(anywhere,) * 3,
        scratch_shapes=scratch,
        compiler_params=pltpu.CompilerParams(
            collective_id=0, has_side_effects=True, vmem_limit_bytes=32 << 20
        ),
    )(*[pltpu.with_memory_space_constraint(operand, pltpu.HBM) for operand in operands])
    output, feature_grad, weight_grad = pl.pallas_call(
        emit,
        out_shape=results,
        in_specs=[anywhere] * 3,
        out_specs=(anywhere,) * 3,
        scratch_shapes=[dma((3,))],
    )(*[pltpu.with_memory_space_constraint(out, pltpu.VMEM) for out in outs])
    return output.reshape(1024, BS), feature_grad.reshape(256, BS), weight_grad.reshape(BS, BS)


def solution(mesh):
    placed = (
        P("dom", "rep"),
        P("dom", "rep", None, None),
        P(("rep", "dom"), None),
        P(),
        P(),
        P("dom", None),
    )
    return jax.shard_map(
        body,
        mesh=mesh,
        in_specs=placed,
        out_specs=(P("dom", None), P(("rep", "dom"), None), P()),
        check_vma=False,
    )
```

time: 944 us -> 65 us (0.07)
  waiting for transfers between devices: 881 us -> 0 us
  Pallas kernels: 0 us -> 64.3 us
  blocking collectives: 28 us -> 0 us
  between operations: 13.8 us -> 0.64 us
    psum x1 -> x0, waiting for transfers between devices: 467 us -> none  [body(): weight_grad = lax.psum(weight_part, 'dom')]
    reduce_scatter x1 -> x0, waiting for transfers between devices: 300 us -> none  [body(): lax.psum_scatter(contrib, 'dom', scatter_dimension=0, tiled=True)]
    all_gather x1 -> x0, waiting for transfers between devices: 114 us -> none  [body(): lax.all_gather(features, 'dom', axis=0, tiled=True)]
    pallas_call x0 -> x2, Pallas kernels: none -> 64.3 us  [the longest x1 63.5 us: body(): pl.pallas_call(kernel, out_shape=results, in_specs=[anywhere] * 6, out_sp...]
    psum x1 -> x0, blocking collectives: 28 us -> none  [body(): summed = lax.psum(partial_sum, 'rep')]
  transfers between devices with their start and end apart: 3 -> 0, of which waited for: 3 -> 0; matrix products, arithmetic and copies ran while one was open for 1% -> 0% of each run, Pallas kernels for 0% -> 0%
where the time goes in v2:
time: 65 us; the launch traced here: 64.9 us
  Pallas kernels  64.3 us (99%)
    pallas_call x1, Pallas kernels, body(): pl.pallas_call(kernel, out_shape=results, in_specs=[anywhere] * 6, out_sp...  63.5 us

profile of v2, /device:TPU:1, one launch (start us, length us, event | category | flops | bytes accessed | tf_op | source)
XLA Modules:
  0.0 64.9 jit_solution(4770797005997095807)
XLA Ops:
  0.6 63.5 %shard_map.85 = (bf16[8,128,128]{2,1,0:T(8,128)(2,1)S(1)}, f32[2,128,128]{2,1,0:T(8,128)S(1)}, f32[2,64,128]{2,1,0:T(8,128)S(1)}) custom-call(s32[2,8]{1,0:T(2,128)} %bitcast.11, bf16[16,128,128]{2,1,0:T(8,128)(2,1)} %bitcast.8, bf16[2,128,128]{2,1,0:T(8,128)(2,1)} %bitcast.10, bf16[128,128]{1,0:T(8,128)(2,1)} %weight_ref.1, f32[1,128]{1,0:T(1,128)} %bitcast.12, ...), custom_call_target="tpu_custom_call" | custom-call | tf_op jit(solution)/shard_map/pallas_call | solution.py:443
  64.1 0.8 %shard_map.86 = (bf16[8,128,128]{2,1,0:T(8,128)(2,1)}, f32[2,128,128]{2,1,0:T(8,128)}, f32[2,64,128]{2,1,0:T(8,128)}) custom-call(bf16[8,128,128]{2,1,0:T(8,128)(2,1)S(1)} %get-tuple-element.9.out_in, f32[2,128,128]{2,1,0:T(8,128)S(1)} %get-tuple-element.10.fgrad_in, f32[2,64,128]{2,1,0:T(8,128)S(1)} %get-tuple-element.11.wgrad_in), custom_call_target="tpu_custom_call" | custom-call | tf_op jit(solution)/shard_map/pallas_call | solution.py:453

commit v3 on v2

--- a/solution.py
+++ b/solution.py
@@ -17,12 +17,12 @@
     cols_ref, vals_ref, feat_ref, weight_ref, bias_ref, cot_ref,
     out_ref, fgrad_ref, wgrad_ref,
     cols_s, first_s, next_s,
-    vals_v, vals_t, weight_v, bias_v, cot_v, first_v,
-    quart, part, part_in, agg, out_v,
+    vals_v, vals_sib, vals_t, weight_v, bias_v, cot_v, first_v,
+    quart, cross, cross_in, part, part_in, agg, out_v,
     wpart, wsib, wa, wb, wr, wfull,
     acc, acc_b, acc_sib,
     dense, relay_in, final_in, summed, near_in, fg_v,
-    load_sem, send_sem, ag_sem, agsib_sem, tab_sem, rep_sem, repag_sem, w_sem, accsib_sem,
+    load_sem, send_sem, ag_sem, cross_sem, vals_sem, tab_sem, rep_sem, repag_sem, w_sem, accsib_sem,
     relay_sem, final_sem, near_sem,
 ):
     rep = lax.axis_index("rep")
@@ -95,16 +95,12 @@
     def to_axis(i, **where):
         send(shard(i), shard(i), ag_sem.at[i], device(**where), 1, 2)
 
-    def to_sib(i):
-        send(shard(i), shard(i), agsib_sem, sib, 0, 2)
-
     def along_b(da, dz):
         i = spot(da, 0, dz)
         to_axis(i, db=1)
         to_axis(i, db=3)
         if (da, dz) in DIRECT:
             to_axis(i, db=2)
-        to_sib(i)
 
     along_b(0, 0)
     for da, dz in near:
@@ -119,7 +115,12 @@
     first = jnp.full((1, 128), 16, jnp.int32)
     for t in reversed(range(16)):
         first = jnp.where(lane == column[t], t, first)
-    first_v[0] = first
+    spots = jnp.zeros((1, 128), jnp.int32)
+    for row in range(8):
+        for k in range(2):
+            spots = jnp.where(lane == row * 2 + k, lax.rem(cols_s[k, row], 128), spots)
+    first_v[0, 0] = first
+    first_v[0, 1] = spots
     first_copy = pltpu.make_async_remote_copy(
         src_ref=first_v.at[0], dst_ref=first_v.at[1], send_sem=send_sem.at[3], recv_sem=tab_sem,
         device_id=sib, device_id_type=MESH,
@@ -137,7 +138,6 @@
             arrive(shard(i), ag_sem.at[i])
             if (da, dz) not in DIRECT:
                 send(half(i, h), half(i, h), half_sem(i, h), device(db=onward), 1, 1)
-            to_sib(i)
 
     def opposite(da, dz):
         i = spot(da, 2, dz)
@@ -146,9 +146,9 @@
         else:
             arrive(half(i, 0), half_sem(i, 0))
             arrive(half(i, 1), half_sem(i, 1))
-        to_sib(i)
 
     load_vals.wait()
+    send(vals_v, vals_sib, vals_sem, sib, 0, 16)
     todo = list(range(16))
 
     def transpose(n):
@@ -189,6 +189,7 @@
     acc[16] = jnp.zeros((BS, BS), F32)
     acc_b[16] = jnp.zeros((BS, BS), BF16)
     acc_sib[16] = jnp.zeros((BS, BS), BF16)
+    quart[128] = jnp.zeros((BS, BS), BF16)
     arrive(first_v.at[1], tab_sem)
     table_copy = pltpu.make_async_copy(first_v, first_s, load_sem.at[6])
     table_copy.start()
@@ -198,36 +199,54 @@
     opposite(1, 1)
     opposite(3, 1)
     opposite(2, 1)
-    arrive(quart.at[pl.ds(0, 64)], agsib_sem)
-
-    def row_sum(row):
-        left = jnp.dot(vals_v[row * 2], quart[lax.rem(cols_s[0, row], 128)], preferred_element_type=F32)
-        right = jnp.dot(vals_v[row * 2 + 1], quart[lax.rem(cols_s[1, row], 128)], preferred_element_type=F32)
-        return left + right
-
+    arrive(vals_sib, vals_sem)
+    table_copy.wait()
+
+    def row_sum(vals, side, row):
+        held = []
+        for k in range(2):
+            spot_at = first_s[side, 1, 0, row * 2 + k]
+            held.append(quart[jnp.where((spot_at // 2) % 2 == c, spot_at, 128)])
+        wide = jnp.concatenate([vals[row * 2], vals[row * 2 + 1]], axis=1)
+        return jnp.dot(wide, jnp.concatenate(held, axis=0), preferred_element_type=F32)
+
+    def targets(j):
+        return [(k, ((rep + k) % 4) * 2 + j) for k in ORDER]
+
+    for j in range(2):
+        for k, row in targets(j):
+            cross[k, j] = row_sum(vals_sib, 1, row)
+        for k in ORDER:
+            send(cross.at[k, j], cross_in.at[k, j], cross_sem.at[k, j], sib, 0, 2)
     own_sum = []
     for j in range(2):
+        totals = [row_sum(vals_v, 0, row) for _, row in targets(j)]
         for k in ORDER:
-            total = row_sum(((rep + k) % 4) * 2 + j)
+            arrive(cross_in.at[k, j], cross_sem.at[k, j])
+        for k, total in zip(ORDER, totals):
+            total = total + cross_in[k, j]
             if k == 0:
                 own_sum.append(total)
             else:
-                part[k, j] = total.astype(BF16)
-                send(part.at[k, j], part_in.at[k, j], rep_sem.at[k, j], device(drep=k))
-
-    def reduce_rep(j):
+                part[k, j] = total.astype(BF16).reshape(2, 64, BS)
+        for q in range(2):
+            for k in (2, 1, 3):
+                send(part.at[k, j, q], part_in.at[k, j, q], rep_sem.at[k - 1, j * 2 + q], device(drep=k), 0, 0.5)
+
+    def reduce_rep(j, q):
         for k in (1, 3, 2):
-            arrive(part_in.at[k, j], rep_sem.at[k, j])
-        total = own_sum[j] + (
-            part_in[1, j].astype(F32) + part_in[3, j].astype(F32) + part_in[2, j].astype(F32)
+            arrive(part_in.at[k, j, q], rep_sem.at[k - 1, j * 2 + q])
+        total = own_sum[j][q * 64 : q * 64 + 64] + (
+            part_in[1, j, q].astype(F32) + part_in[3, j, q].astype(F32) + part_in[2, j, q].astype(F32)
         )
-        agg[rep * 2 + j] = total.astype(BF16)
+        agg[rep * 2 + j, q] = total.astype(BF16)
         for k in (2, 1, 3):
-            send(agg.at[rep * 2 + j], agg.at[rep * 2 + j], repag_sem.at[k, j], device(drep=k))
+            piece = agg.at[rep * 2 + j, q]
+            send(piece, piece, repag_sem.at[k - 1, j * 2 + q], device(drep=k), 0, 0.5)
 
     def layer(pos):
         row = rows[pos]
-        mine = agg[row]
+        mine = agg[row].reshape(BS, BS)
         hidden = jnp.dot(mine, weight_v[...], preferred_element_type=F32) + bias_v[...]
         gate = jax.nn.sigmoid(hidden)
         out_v[row] = (hidden * gate).astype(BF16)
@@ -272,19 +291,21 @@
     load_weight.wait()
     load_bias.wait()
     load_cot.wait()
-    reduce_rep(0)
+    reduce_rep(0, 0)
+    reduce_rep(0, 1)
     product = layer(7)
-    reduce_rep(1)
+    reduce_rep(1, 0)
+    reduce_rep(1, 1)
     product = product + layer(6)
     wpart[0] = product[:64]
     wpart[1] = product[64:]
     send(wpart.at[1 - c], wsib, w_sem.at[0], sib)
     for n, (k, j) in enumerate(arrivals):
-        arrive(agg.at[rows[5 - n]], repag_sem.at[k, j])
+        for q in range(2):
+            arrive(agg.at[rows[5 - n], q], repag_sem.at[k - 1, j * 2 + q])
         layer(5 - n)
         if n == 1:
             w_stage_near()
-    table_copy.wait()
     arrive(acc_sib.at[pl.ds(0, 16)], accsib_sem)
 
     def place(ob, oa, zz):
@@ -295,7 +316,7 @@
             i = flat((pa + oa) % 4, (pb + ob) % 4, zz)
             for blk in range(2):
                 j = (i * 2 + c) * 2 + blk
-                dense[place(ob, oa, zz) + blk] = acc_b[first_s[0, 0, j]] + acc_sib[first_s[1, 0, j]]
+                dense[place(ob, oa, zz) + blk] = acc_b[first_s[0, 0, 0, j]] + acc_sib[first_s[1, 0, 0, j]]
 
     def to_b(oa, ob, zz):
         side = 0 if ob == 1 else 1
@@ -323,6 +344,7 @@
         if n < 3:
             to_b(ORDER[n + 1], 1, 1)
             to_b(ORDER[n + 1], 3, 0)
+    w_stage_rep()
     for oa in ORDER:
         build(0, oa)
 
@@ -340,8 +362,6 @@
             if oa or dz:
                 slot = oa * 2 + dz
                 send(summed.at[oa, (z + dz) % 2], near_in.at[slot], near_sem.at[slot], device(da=oa, dz=dz), 2, 2)
-        if oa == 2:
-            w_stage_rep()
     w_stage_sib()
     total = fg_v[z]
     for oa in ORDER:
@@ -357,8 +377,8 @@
     wgrad_copy = pltpu.make_async_copy(wfull, wgrad_ref, load_sem.at[9])
     wgrad_copy.start()
     for group, blocks in enumerate(sent):
-        assert blocks <= 128
-        ref = quart.at[pl.ds(0, blocks)]
+        assert blocks <= 128 and blocks == int(blocks)
+        ref = quart.at[pl.ds(0, int(blocks))]
         pltpu.make_async_remote_copy(
             src_ref=ref, dst_ref=ref, send_sem=send_sem.at[group], recv_sem=tab_sem, device_id=sib, device_id_type=MESH
         ).wait_send()
@@ -386,18 +406,21 @@
     block = (BS, BS)
     scratch = [
         pltpu.SMEM((2, 8), jnp.int32),
-        pltpu.SMEM((2, 1, 128), jnp.int32),
+        pltpu.SMEM((2, 2, 1, 128), jnp.int32),
         pltpu.SMEM((16,), jnp.int32),
+        vmem((16, *block), BF16),
         vmem((16, *block), BF16),
         vmem((16, *block), BF16),
         vmem(block, BF16),
         vmem((1, BS), F32),
         vmem((8, *block), BF16),
-        vmem((2, 1, 128), jnp.int32),
-        vmem((128, *block), BF16),
-        vmem((4, 2, *block), BF16),
-        vmem((4, 2, *block), BF16),
-        vmem((8, *block), BF16),
+        vmem((2, 2, 1, 128), jnp.int32),
+        vmem((129, *block), BF16),
+        vmem((4, 2, *block), F32),
+        vmem((4, 2, *block), F32),
+        vmem((4, 2, 2, 64, BS), BF16),
+        vmem((4, 2, 2, 64, BS), BF16),
+        vmem((8, 2, 64, BS), BF16),
         vmem((8, *block), BF16),
         vmem((2, 64, BS), F32),
         vmem((64, BS), F32),
@@ -417,10 +440,11 @@
         dma((10,)),
         dma((4,)),
         dma((64,)),
+        dma((4, 2)),
         dma,
         dma,
-        dma((4, 2)),
-        dma((4, 2)),
+        dma((3, 4)),
+        dma((3, 4)),
         dma((15,)),
         dma,
         dma((2, 4)),

time: 65 us -> 64.1 us (0.986)
  Pallas kernels: 64.3 us -> 63.4 us
    pallas_call x1, Pallas kernels: 63.5 us -> 62.6 us  [body(): pl.pallas_call(kernel, out_shape=results, in_specs=[anywhere] * 6, out_sp...]
where the time goes in v3:
time: 64.1 us; the launch traced here: 64 us
  Pallas kernels  63.4 us (99%)
    pallas_call x1, Pallas kernels, body(): pl.pallas_call(kernel, out_shape=results, in_specs=[anywhere] * 6, out_sp...  62.6 us

profile of v3, /device:TPU:1, one launch (start us, length us, event | category | flops | bytes accessed | tf_op | source)
XLA Modules:
  0.0 64.0 jit_solution(15048224877893804667)
XLA Ops:
  0.6 62.6 %shard_map.85 = (bf16[8,128,128]{2,1,0:T(8,128)(2,1)S(1)}, f32[2,128,128]{2,1,0:T(8,128)S(1)}, f32[2,64,128]{2,1,0:T(8,128)S(1)}) custom-call(s32[2,8]{1,0:T(2,128)} %bitcast.11, bf16[16,128,128]{2,1,0:T(8,128)(2,1)} %bitcast.8, bf16[2,128,128]{2,1,0:T(8,128)(2,1)} %bitcast.10, bf16[128,128]{1,0:T(8,128)(2,1)} %weight_ref.1, f32[1,128]{1,0:T(1,128)} %bitcast.12, ...), custom_call_target="tpu_custom_call" | custom-call | tf_op jit(solution)/shard_map/pallas_call | solution.py:467
  63.2 0.8 %shard_map.86 = (bf16[8,128,128]{2,1,0:T(8,128)(2,1)}, f32[2,128,128]{2,1,0:T(8,128)}, f32[2,64,128]{2,1,0:T(8,128)}) custom-call(bf16[8,128,128]{2,1,0:T(8,128)(2,1)S(1)} %get-tuple-element.9.out_in, f32[2,128,128]{2,1,0:T(8,128)S(1)} %get-tuple-element.10.fgrad_in, f32[2,64,128]{2,1,0:T(8,128)S(1)} %get-tuple-element.11.wgrad_in), custom_call_target="tpu_custom_call" | custom-call | tf_op jit(solution)/shard_map/pallas_call | solution.py:477

commit v4 on v3

--- a/solution.py
+++ b/solution.py
@@ -23,7 +23,7 @@
     acc, acc_b, acc_sib,
     dense, relay_in, final_in, summed, near_in, fg_v,
     load_sem, send_sem, ag_sem, cross_sem, vals_sem, tab_sem, rep_sem, repag_sem, w_sem, accsib_sem,
-    relay_sem, final_sem, near_sem,
+    relay_sem, final_sem, last_sem, near_sem,
 ):
     rep = lax.axis_index("rep")
     dom = lax.axis_index("dom")
@@ -103,7 +103,7 @@
             to_axis(i, db=2)
 
     along_b(0, 0)
-    for da, dz in near:
+    for da, dz in ((0, 1), (1, 0), (3, 0), (2, 0), (1, 1), (3, 1)):
         to_axis(own, da=da, dz=dz)
 
     arrivals = [(k, j) for j in range(2) for k in (1, 3, 2)]
@@ -130,6 +130,8 @@
     def near_shard(da, dz):
         i = spot(da, 0, dz)
         arrive(shard(i), ag_sem.at[i])
+        if (da, dz) == (0, 1):
+            to_axis(i, da=2)
         along_b(da, dz)
 
     def beside(da, dz):
@@ -157,9 +159,9 @@
             vals_t[t] = vals_v[rows[t // 2] * 2 + t % 2].T
 
     transpose(4)
+    near_shard(0, 1)
     near_shard(1, 0)
     near_shard(3, 0)
-    near_shard(0, 1)
     beside(0, 0)
     near_shard(2, 0)
     near_shard(1, 1)
@@ -335,43 +337,68 @@
             to_b(oa, 1, 1)
             to_b(oa, 3, 0)
     w_stage_b()
-    for n, oa in enumerate(ORDER):
+    other = 1 - z
+
+    def to_b_last(ob, zz):
+        side = (ob - 1) // 2
+        send(
+            dense.at[pl.ds(place(ob, 0, zz), 2)], final_in.at[side, 0, zz], last_sem.at[side, zz], device(db=ob), 2, 2
+        )
+
+    def add_relay(side, ob, oa, zz):
+        arrive(relay_in.at[side, oa], relay_sem.at[side, oa])
+        at = pl.ds(place(ob, oa, zz), 2)
+        dense[at] = (dense[at].astype(F32) + relay_in[side, oa].astype(F32)).astype(BF16)
+
+    for n, oa in enumerate(ORDER[:3]):
         for side, ob, zz in ((0, 1, 0), (1, 3, 1)):
-            arrive(relay_in.at[side, oa], relay_sem.at[side, oa])
-            at = pl.ds(place(ob, oa, zz), 2)
-            dense[at] = (dense[at].astype(F32) + relay_in[side, oa].astype(F32)).astype(BF16)
+            add_relay(side, ob, oa, zz)
             to_b(oa, ob, zz)
-        if n < 3:
+        if n < 2:
             to_b(ORDER[n + 1], 1, 1)
             to_b(ORDER[n + 1], 3, 0)
+    to_b_last(3 - 2 * other, other)
+    add_relay(other, 1 + 2 * other, 0, other)
+    to_b_last(1 + 2 * other, other)
+    to_b_last(3 - 2 * z, z)
+    add_relay(z, 1 + 2 * z, 0, z)
+    to_b_last(1 + 2 * z, z)
     w_stage_rep()
     for oa in ORDER:
         build(0, oa)
 
-    for oa in ORDER:
+    def sum_b(oa, zz):
+        return dense[pl.ds(place(0, oa, zz), 2)].astype(F32) + (
+            final_in[0, oa, zz].astype(F32) + final_in[1, oa, zz].astype(F32)
+        )
+
+    def to_near(oa, dz):
+        slot = oa * 2 + dz
+        send(summed.at[oa, (z + dz) % 2], near_in.at[slot], near_sem.at[slot], device(da=oa, dz=dz), 2, 2)
+
+    for oa in ORDER[:3]:
         for side in range(2):
             arrive(final_in.at[side, oa], final_sem.at[side, oa])
         for zz in range(2):
-            total = dense[pl.ds(place(0, oa, zz), 2)].astype(F32) + (
-                final_in[0, oa, zz].astype(F32) + final_in[1, oa, zz].astype(F32)
-            )
-            summed[oa, zz] = total.astype(BF16)
-            if oa == 0:
-                fg_v[zz] = total
-        for dz in (1, 0):
-            if oa or dz:
-                slot = oa * 2 + dz
-                send(summed.at[oa, (z + dz) % 2], near_in.at[slot], near_sem.at[slot], device(da=oa, dz=dz), 2, 2)
+            summed[oa, zz] = sum_b(oa, zz).astype(BF16)
+        to_near(oa, 1)
+        to_near(oa, 0)
+    for side in range(2):
+        arrive(final_in.at[side, 0, other], last_sem.at[side, other])
+    summed[0, other] = sum_b(0, other).astype(BF16)
+    to_near(0, 1)
     w_stage_sib()
-    total = fg_v[z]
+    for side in range(2):
+        arrive(final_in.at[side, 0, z], last_sem.at[side, z])
+    total = sum_b(0, z)
     for oa in ORDER:
         for dz in (0, 1):
             if oa or dz:
                 slot = oa * 2 + dz
                 arrive(near_in.at[slot], near_sem.at[slot])
                 total = total + near_in[slot].astype(F32)
-    fg_v[2] = total
-    fgrad_copy = pltpu.make_async_copy(fg_v.at[2], fgrad_ref, load_sem.at[8])
+    fg_v[...] = total
+    fgrad_copy = pltpu.make_async_copy(fg_v, fgrad_ref, load_sem.at[8])
     fgrad_copy.start()
     arrive(wfull.at[1 - c], w_sem.at[14])
     wgrad_copy = pltpu.make_async_copy(wfull, wgrad_ref, load_sem.at[9])
@@ -436,7 +463,7 @@
         vmem((2, 4, 2, 2, *block), BF16),
         vmem((4, 2, 2, *block), BF16),
         vmem((8, 2, *block), BF16),
-        vmem((3, 2, *block), F32),
+        vmem((2, *block), F32),
         dma((10,)),
         dma((4,)),
         dma((64,)),
@@ -449,6 +476,7 @@
         dma,
         dma((2, 4)),
         dma((2, 4)),
+        dma((2, 2)),
         dma((8,)),
     ]
     results = (

time: 64.1 us -> 64.9 us (1.012)
  Pallas kernels: 63.4 us -> 64.1 us
    pallas_call x1, Pallas kernels: 62.6 us -> 63.3 us  [body(): pl.pallas_call(kernel, out_shape=results, in_specs=[anywhere] * 6, out_sp...]
where the time goes in v4:
time: 64.9 us; the launch traced here: 64.8 us
  Pallas kernels  64.1 us (99%)
    pallas_call x1, Pallas kernels, body(): pl.pallas_call(kernel, out_shape=results, in_specs=[anywhere] * 6, out_sp...  63.3 us

profile of v4, /device:TPU:1, one launch (start us, length us, event | category | flops | bytes accessed | tf_op | source)
XLA Modules:
  0.0 64.8 jit_solution(3339505911617205777)
XLA Ops:
  0.6 63.3 %shard_map.85 = (bf16[8,128,128]{2,1,0:T(8,128)(2,1)S(1)}, f32[2,128,128]{2,1,0:T(8,128)S(1)}, f32[2,64,128]{2,1,0:T(8,128)S(1)}) custom-call(s32[2,8]{1,0:T(2,128)} %bitcast.11, bf16[16,128,128]{2,1,0:T(8,128)(2,1)} %bitcast.8, bf16[2,128,128]{2,1,0:T(8,128)(2,1)} %bitcast.10, bf16[128,128]{1,0:T(8,128)(2,1)} %weight_ref.1, f32[1,128]{1,0:T(1,128)} %bitcast.12, ...), custom_call_target="tpu_custom_call" | custom-call | tf_op jit(solution)/shard_map/pallas_call | solution.py:495
  64.0 0.8 %shard_map.86 = (bf16[8,128,128]{2,1,0:T(8,128)(2,1)}, f32[2,128,128]{2,1,0:T(8,128)}, f32[2,64,128]{2,1,0:T(8,128)}) custom-call(bf16[8,128,128]{2,1,0:T(8,128)(2,1)S(1)} %get-tuple-element.9.out_in, f32[2,128,128]{2,1,0:T(8,128)S(1)} %get-tuple-element.10.fgrad_in, f32[2,64,128]{2,1,0:T(8,128)S(1)} %get-tuple-element.11.wgrad_in), custom_call_target="tpu_custom_call" | custom-call | tf_op jit(solution)/shard_map/pallas_call | solution.py:505
